TPU v7x, 32 devices: a whole 2x2x4 slice. The times are simulated.
32 devices in a mesh: dp: 4 (over x, core), seq: 2 (over y), tensor: 4 (over z).
Axes of the slice: x: 2, y: 2, z: 4, core: 2. Of those that a mesh axis runs over, the one named last changes fastest.
Arguments:
- tokens: bfloat16 [8, 1024, 768], P('dp', 'seq'), may hold values from -6 to 6
- segments: int32 [8, 1024], P('dp'), may hold values from 0 to 2, never falling along the last dimension, each value on 1 to 512 neighbouring positions
- projections: bfloat16 [3, 768, 768], P(None, ('dp', 'seq'), 'tensor'), may hold values from -0.21875 to 0.21875
- offsets: bfloat16 [2, 12, 64], P(None, 'tensor', ('dp', 'seq')), may hold values from -3 to 3
- mixing: bfloat16 [768, 768], P('tensor', ('dp', 'seq')), may hold values from -2.5 to 2.5
- upward: bfloat16 [768, 3072], P(('dp', 'seq'), 'tensor'), may hold values from -0.21875 to 0.21875
- thresholds: bfloat16 [48, 64], P('tensor', ('dp', 'seq')), may hold values from -3 to 3
- downward: bfloat16 [3072, 768], P('tensor', ('dp', 'seq')), may hold values from -0.109375 to 0.109375
- scales: bfloat16 [2, 768], P(None, ('dp', 'seq')), may hold values from 0.099609375 to 1.8984375
- shifts: bfloat16 [2, 768], P(None, ('dp', 'seq')), may hold values from -2 to 2
- biases: bfloat16 [2, 768], P(None, ('dp', 'seq')), may hold values from -2 to 2
- cotangent: bfloat16 [8, 1024, 768], P('dp', 'seq'), may hold values from -6 to 6
Outputs:
- result: bfloat16 [8, 1024, 768], P('dp', 'seq')
- tokens_grad: bfloat16 [8, 1024, 768], P('dp', 'seq')
- projections_grad: float32 [3, 768, 768], P(None, ('dp', 'seq'), 'tensor')
- offsets_grad: float32 [2, 12, 64], P(None, 'tensor', ('dp', 'seq'))
- mixing_grad: float32 [768, 768], P('tensor', ('dp', 'seq'))
- upward_grad: float32 [768, 3072], P(('dp', 'seq'), 'tensor')
- thresholds_grad: float32 [48, 64], P('tensor', ('dp', 'seq'))
- downward_grad: float32 [3072, 768], P('tensor', ('dp', 'seq'))
- scales_grad: float32 [2, 768], P(None, ('dp', 'seq'))
- shifts_grad: float32 [2, 768], P(None, ('dp', 'seq'))
- biases_grad: float32 [2, 768], P(None, ('dp', 'seq'))
Inputs may be any that keep to these rules, and one draw needn't show every extreme that they name: `segments`: ids never fall along a sequence; each document holds 1 to 512 tokens, and one holds exactly 512.
All inputs are finite; a program needn't handle non-finite values.
Results may differ from a plain program's by a relative error of at most 0.012.
Values may be sent and summed in bfloat16 or wider, within the bound.
A program may use at most 128 MiB of HBM per device.

v0:
```python
import jax
import jax.numpy as jnp
from jax import lax
from jax.sharding import PartitionSpec as P


def norm_rows(values, gain_row, shift_row):
    average = jnp.mean(values, axis=-1, keepdims=True)
    centered = values - average
    variance = jnp.mean(centered * centered, axis=-1, keepdims=True)
    return centered * lax.rsqrt(variance + 1e-05) * gain_row + shift_row


def gelu_tanh(values):
    return (
        0.5
        * values
        * (1.0 + jnp.tanh(0.7978845608028654 * (values + 0.044715 * values * values * values)))
    )


def head_scores(query_head, key_head, allowed):
    scores = (
        jnp.einsum("qe,ke->qk", query_head, key_head, preferred_element_type=jnp.float32) * 0.125
    )
    return jnp.where(allowed, scores, -1e30)


def accumulate(running, addition):
    return addition if running is None else running + addition


def per_device(
    tokens,
    segments,
    projections,
    offsets,
    mixing,
    upward,
    thresholds,
    downward,
    scales,
    shifts,
    biases,
    cotangent,
):
    micro = tokens.shape[0]
    block_len = tokens.shape[1]
    seq_len = segments.shape[1]
    head_size = offsets.shape[2] * lax.axis_size(("dp", "seq"))
    start = lax.axis_index("seq") * block_len
    query_pos = start + jnp.arange(block_len, dtype=jnp.int32)
    key_pos = jnp.arange(seq_len, dtype=jnp.int32)
    saved = []
    results = []
    for batch_index in range(micro):
        gathered = (
            lax.all_gather(projections, ("dp", "seq"), axis=1, tiled=True),
            lax.all_gather(offsets, ("dp", "seq"), axis=2, tiled=True),
            lax.all_gather(mixing, ("dp", "seq"), axis=1, tiled=True),
            lax.all_gather(upward, ("dp", "seq"), axis=0, tiled=True),
            lax.all_gather(thresholds, ("dp", "seq"), axis=1, tiled=True),
            lax.all_gather(downward, ("dp", "seq"), axis=1, tiled=True),
            lax.all_gather(scales, ("dp", "seq"), axis=1, tiled=True),
            lax.all_gather(shifts, ("dp", "seq"), axis=1, tiled=True),
            lax.all_gather(biases, ("dp", "seq"), axis=1, tiled=True),
        )
        (
            entry_weights,
            entry_offsets,
            mixer_weights,
            upward_full,
            threshold_full,
            downward_full,
            scale_full,
            shift_full,
            biases_full,
        ) = gathered
        scale_rows = scale_full.astype(jnp.float32)
        shift_rows = shift_full.astype(jnp.float32)
        bias_rows = biases_full.astype(jnp.float32)
        offset_rows = entry_offsets.astype(jnp.float32).reshape(2, -1)
        inputs = tokens[batch_index].astype(jnp.float32)
        normed = norm_rows(inputs, scale_rows[0], shift_rows[0]).astype(jnp.bfloat16)
        stacked = jnp.einsum(
            "cd,tde->tce", normed, entry_weights, preferred_element_type=jnp.float32
        )
        query_b = (stacked[0] + offset_rows[0]).astype(jnp.bfloat16)
        key_b = stacked[1].astype(jnp.bfloat16)
        value_b = (stacked[2] + offset_rows[1]).astype(jnp.bfloat16)
        key_full, value_full = (
            lax.all_gather(key_b, "seq", axis=0, tiled=True),
            lax.all_gather(value_b, "seq", axis=0, tiled=True),
        )
        seg_row = segments[batch_index]
        own_seg = lax.dynamic_slice_in_dim(seg_row, start, block_len)
        allowed = (key_pos[None, :] <= query_pos[:, None]) & (seg_row[None, :] == own_seg[:, None])
        head_count = query_b.shape[1] // head_size
        pieces = []
        totals = []
        for head_index in range(head_count):
            columns = slice(head_index * head_size, (head_index + 1) * head_size)
            scores = head_scores(query_b[:, columns], key_full[:, columns], allowed)
            log_total = jax.nn.logsumexp(scores, axis=1, keepdims=True)
            weights_b = jnp.exp(scores - log_total).astype(jnp.bfloat16)
            pieces.append(
                jnp.dot(weights_b, value_full[:, columns], preferred_element_type=jnp.float32)
            )
            totals.append(log_total)
        attended = jnp.concatenate(pieces, axis=1).astype(jnp.bfloat16)
        branch = lax.psum(
            jnp.dot(attended, mixer_weights, preferred_element_type=jnp.float32), "tensor"
        )
        hidden = inputs + branch + bias_rows[0]
        normed2 = norm_rows(hidden, scale_rows[1], shift_rows[1]).astype(jnp.bfloat16)
        pre_act = jnp.dot(
            normed2, upward_full, preferred_element_type=jnp.float32
        ) + threshold_full.astype(jnp.float32).reshape(-1)
        activated = gelu_tanh(pre_act).astype(jnp.bfloat16)
        lifted = lax.psum(
            jnp.dot(activated, downward_full, preferred_element_type=jnp.float32).astype(
                jnp.bfloat16
            ),
            "tensor",
        ).astype(jnp.float32)
        results.append((hidden + lifted + bias_rows[1]).astype(jnp.bfloat16))
        kept_keys = (key_b, value_b)
        saved.append(
            (
                inputs,
                normed,
                query_b,
                kept_keys,
                allowed,
                totals,
                attended,
                hidden,
                normed2,
                pre_act,
                activated,
            )
        )
    entry_acc = None
    offset_acc = None
    mixer_acc = None
    upward_acc = None
    threshold_acc = None
    downward_acc = None
    scale_acc = None
    shift_acc = None
    bias_acc = None
    input_grads = []
    for batch_index in range(micro):
        gathered = (
            lax.all_gather(projections, ("dp", "seq"), axis=1, tiled=True),
            lax.all_gather(offsets, ("dp", "seq"), axis=2, tiled=True),
            lax.all_gather(mixing, ("dp", "seq"), axis=1, tiled=True),
            lax.all_gather(upward, ("dp", "seq"), axis=0, tiled=True),
            lax.all_gather(thresholds, ("dp", "seq"), axis=1, tiled=True),
            lax.all_gather(downward, ("dp", "seq"), axis=1, tiled=True),
            lax.all_gather(scales, ("dp", "seq"), axis=1, tiled=True),
            lax.all_gather(shifts, ("dp", "seq"), axis=1, tiled=True),
            lax.all_gather(biases, ("dp", "seq"), axis=1, tiled=True),
        )
        (
            entry_weights,
            entry_offsets,
            mixer_weights,
            upward_full,
            threshold_full,
            downward_full,
            scale_full,
            shift_full,
            biases_full,
        ) = gathered
        scale_rows = scale_full.astype(jnp.float32)
        shift_rows = shift_full.astype(jnp.float32)
        (
            inputs,
            normed,
            query_b,
            kept_keys,
            allowed,
            totals,
            attended,
            hidden,
            normed2,
            pre_act,
            activated,
        ) = saved[batch_index]
        grad_out = cotangent[batch_index].astype(jnp.float32)
        grad_out_b = grad_out.astype(jnp.bfloat16)
        downward_acc = accumulate(
            downward_acc,
            jnp.einsum("cf,cd->fd", activated, grad_out_b, preferred_element_type=jnp.float32),
        )
        grad_act = jnp.einsum(
            "cd,fd->cf", grad_out_b, downward_full, preferred_element_type=jnp.float32
        )
        unused, gelu_back = jax.vjp(gelu_tanh, pre_act)
        grad_pre = gelu_back(grad_act)[0].astype(jnp.bfloat16)
        threshold_acc = accumulate(threshold_acc, jnp.sum(grad_pre.astype(jnp.float32), axis=0))
        upward_acc = accumulate(
            upward_acc,
            jnp.einsum("cd,cf->df", normed2, grad_pre, preferred_element_type=jnp.float32),
        )
        grad_normed2 = lax.psum(
            jnp.einsum("cf,df->cd", grad_pre, upward_full, preferred_element_type=jnp.float32),
            "tensor",
        )
        unused, second_back = jax.vjp(norm_rows, hidden, scale_rows[1], shift_rows[1])
        grad_from_norm, scale_second, shift_second = second_back(grad_normed2)
        grad_hidden = grad_out + grad_from_norm
        grad_hidden_b = grad_hidden.astype(jnp.bfloat16)
        mixer_acc = accumulate(
            mixer_acc,
            jnp.einsum("ce,cd->ed", attended, grad_hidden_b, preferred_element_type=jnp.float32),
        )
        grad_attended = jnp.einsum(
            "cd,ed->ce", grad_hidden_b, mixer_weights, preferred_element_type=jnp.float32
        ).astype(jnp.bfloat16)
        own_keys, own_values = kept_keys
        key_full, value_full = (
            lax.all_gather(own_keys, "seq", axis=0, tiled=True),
            lax.all_gather(own_values, "seq", axis=0, tiled=True),
        )
        head_count = query_b.shape[1] // head_size
        query_grads = []
        key_grads = []
        value_grads = []
        for head_index in range(head_count):
            columns = slice(head_index * head_size, (head_index + 1) * head_size)
            scores = head_scores(query_b[:, columns], key_full[:, columns], allowed)
            probs = jnp.exp(scores - totals[head_index])
            grad_slice = grad_attended[:, columns]
            grad_probs = jnp.einsum(
                "qe,ke->qk", grad_slice, value_full[:, columns], preferred_element_type=jnp.float32
            )
            delta_rows = jnp.sum(probs * grad_probs, axis=1, keepdims=True)
            grad_scores = (probs * (grad_probs - delta_rows)).astype(jnp.bfloat16)
            query_grads.append(
                jnp.einsum(
                    "qk,ke->qe",
                    grad_scores,
                    key_full[:, columns],
                    preferred_element_type=jnp.float32,
                )
                * 0.125
            )
            probs_b = probs.astype(jnp.bfloat16)
            value_grads.append(
                jnp.einsum("qk,qe->ke", probs_b, grad_slice, preferred_element_type=jnp.float32)
            )
            key_grads.append(
                jnp.einsum(
                    "qk,qe->ke",
                    grad_scores,
                    query_b[:, columns],
                    preferred_element_type=jnp.float32,
                )
                * 0.125
            )
        key_grad_full = jnp.concatenate(key_grads, axis=1)
        value_grad_full = jnp.concatenate(value_grads, axis=1)
        key_grad, value_grad = (
            lax.psum_scatter(key_grad_full, "seq", scatter_dimension=0, tiled=True),
            lax.psum_scatter(value_grad_full, "seq", scatter_dimension=0, tiled=True),
        )
        triple = jnp.stack([jnp.concatenate(query_grads, axis=1), key_grad, value_grad]).astype(
            jnp.bfloat16
        )
        triple_sums = jnp.sum(triple.astype(jnp.float32), axis=1)
        offset_acc = accumulate(offset_acc, jnp.stack([triple_sums[0], triple_sums[2]]))
        entry_acc = accumulate(
            entry_acc, jnp.einsum("cd,tce->tde", normed, triple, preferred_element_type=jnp.float32)
        )
        grad_normed = lax.psum(
            jnp.einsum("tce,tde->cd", triple, entry_weights, preferred_element_type=jnp.float32),
            "tensor",
        )
        unused, first_back = jax.vjp(norm_rows, inputs, scale_rows[0], shift_rows[0])
        grad_inputs, scale_first, shift_first = first_back(grad_normed)
        input_grads.append((grad_hidden + grad_inputs).astype(jnp.bfloat16))
        scale_acc = accumulate(scale_acc, jnp.stack([scale_first, scale_second]))
        shift_acc = accumulate(shift_acc, jnp.stack([shift_first, shift_second]))
        bias_acc = accumulate(
            bias_acc, jnp.stack([jnp.sum(grad_hidden, axis=0), jnp.sum(grad_out, axis=0)])
        )
    offset_acc = offset_acc.reshape(entry_offsets.shape)
    threshold_acc = threshold_acc.reshape(threshold_full.shape)
    summed = (
        lax.psum_scatter(entry_acc, ("dp", "seq"), scatter_dimension=1, tiled=True),
        lax.psum_scatter(offset_acc, ("dp", "seq"), scatter_dimension=2, tiled=True),
        lax.psum_scatter(mixer_acc, ("dp", "seq"), scatter_dimension=1, tiled=True),
        lax.psum_scatter(upward_acc, ("dp", "seq"), scatter_dimension=0, tiled=True),
        lax.psum_scatter(threshold_acc, ("dp", "seq"), scatter_dimension=1, tiled=True),
        lax.psum_scatter(downward_acc, ("dp", "seq"), scatter_dimension=1, tiled=True),
        lax.psum_scatter(scale_acc, ("dp", "seq"), scatter_dimension=1, tiled=True),
        lax.psum_scatter(shift_acc, ("dp", "seq"), scatter_dimension=1, tiled=True),
        lax.psum_scatter(bias_acc, ("dp", "seq"), scatter_dimension=1, tiled=True),
    )
    return (
        jnp.stack(results),
        jnp.stack(input_grads),
        summed[0],
        summed[1],
        summed[2],
        summed[3],
        summed[4],
        summed[5],
        summed[6],
        summed[7],
        summed[8],
    )


def solution(mesh):
    placed = (
        P("dp", "seq", None),
        P("dp", None),
        P(None, ("dp", "seq"), "tensor"),
        P(None, "tensor", ("dp", "seq")),
        P("tensor", ("dp", "seq")),
        P(("dp", "seq"), "tensor"),
        P("tensor", ("dp", "seq")),
        P("tensor", ("dp", "seq")),
        P(None, ("dp", "seq")),
        P(None, ("dp", "seq")),
        P(None, ("dp", "seq")),
        P("dp", "seq", None),
    )
    return jax.shard_map(
        per_device,
        mesh=mesh,
        in_specs=placed,
        out_specs=(
            P("dp", "seq", None),
            P("dp", "seq", None),
            P(None, ("dp", "seq"), "tensor"),
            P(None, "tensor", ("dp", "seq")),
            P("tensor", ("dp", "seq")),
            P(("dp", "seq"), "tensor"),
            P("tensor", ("dp", "seq")),
            P("tensor", ("dp", "seq")),
            P(None, ("dp", "seq")),
            P(None, ("dp", "seq")),
            P(None, ("dp", "seq")),
        ),
        check_vma=False,
    )
```

profile of v0, /device:TPU:0, one launch (start us, length us, event | category | flops | bytes accessed | tf_op | source)
XLA Modules:
  0.0 897.6 jit_solution(6401317190653829994)
XLA Ops:
  9.0 13.2 %all-gather.2 = bf16[8,96,2]{1,2,0:T(2,128)(2,1)S(1)} all-gather(bf16[1,96,2]{1,2,0:T(2,128)(2,1)} %bitcast.306), channel_id=1, replica_groups=mesh['dp'=4,'seq'=2,'tensor'=4] {'dp','seq'}, dimensions={0}, use_global_device_ids=true | all-gather | bytes 3456 | tf_op jit(solution)/shard_map/all_gather | solution.py:64
  22.3 10.9 %all-gather.3 = bf16[8,96,2]{1,2,0:T(2,128)(2,1)S(1)} all-gather(bf16[1,96,2]{1,2,0:T(2,128)(2,1)} %bitcast.307), channel_id=1, replica_groups=mesh['dp'=4,'seq'=2,'tensor'=4] {'dp','seq'}, dimensions={0}, use_global_device_ids=true | all-gather | bytes 3456 | tf_op jit(solution)/shard_map/all_gather | solution.py:65
  36.2 12.5 %all_gather.29 = bf16[2,3,64]{1,0,2:T(2,128)(2,1)S(1)} all-gather(bf16[2,3,8]{1,0,2:T(2,128)(2,1)S(1)} %copy.73), channel_id=1, replica_groups=mesh['dp'=4,'seq'=2,'tensor'=4] {'dp','seq'}, dimensions={2}, use_global_device_ids=true | all-gather | bytes 864 | tf_op jit(solution)/shard_map/all_gather | solution.py:59
  49.3 23.8 %all_gather.28 = bf16[3,768,192]{2,0,1:T(4,128)(2,1)S(1)} all-gather(bf16[3,96,192]{2,0,1:T(4,128)(2,1)S(1)} %copy.71), channel_id=1, replica_groups=mesh['dp'=4,'seq'=2,'tensor'=4] {'dp','seq'}, dimensions={1}, use_global_device_ids=true | all-gather | bytes 995328 | tf_op jit(solution)/shard_map/all_gather | solution.py:58
  79.8 8.4 all-gather
  96.4 7.5 all-gather.1
  110.1 15.6 %all_gather.32 = bf16[192,768]{0,1:T(8,128)(2,1)S(1)} all-gather(bf16[192,96]{0,1:T(8,128)(2,1)S(1)} %copy.76), channel_id=1, replica_groups=mesh['dp'=4,'seq'=2,'tensor'=4] {'dp','seq'}, dimensions={1}, use_global_device_ids=true | all-gather | bytes 331776 | tf_op jit(solution)/shard_map/all_gather | solution.py:60
  125.8 8.3 all_gather.74
  134.0 7.9 all_gather.31
  159.0 11.3 %all-gather.4 = bf16[8,96,2]{1,2,0:T(2,128)(2,1)S(1)} all-gather(bf16[1,96,2]{1,2,0:T(2,128)(2,1)S(1)} %bitcast.308), channel_id=1, replica_groups=mesh['dp'=4,'seq'=2,'tensor'=4] {'dp','seq'}, dimensions={0}, use_global_device_ids=true | all-gather | bytes 3456 | tf_op jit(solution)/shard_map/all_gather | solution.py:66
  171.0 16.6 %all_gather.35 = bf16[12,64]{0,1:T(8,128)(2,1)S(1)} all-gather(bf16[12,8]{0,1:T(8,128)(2,1)S(1)} %copy-done.131), channel_id=1, replica_groups=mesh['dp'=4,'seq'=2,'tensor'=4] {'dp','seq'}, dimensions={1}, use_global_device_ids=true | all-gather | bytes 1728 | tf_op jit(solution)/shard_map/all_gather | solution.py:62
  188.4 91.1 %all-reduce.16.cloned.1.call-done = (f32[512,768]{1,0:T(8,128)}, f32[512,768]{1,0:T(8,128)}) async-done(((f32[512,768]{1,0:T(8,128)}, f32[512,768]{1,0:T(8,128)}), (f32[512,768]{1,0:T(8,128)}, f32[512,768]{1,0:T(8,128)})) %all-reduce.16.cloned.1.call-update) | async-done | bytes 3145744 | tf_op jit(solution)/shard_map/psum | solution.py:111
  284.3 3.9 convolution_add_fusion.3
  290.3 4.5 convert_reduce_fusion.5
  301.3 3.9 convolution_convert_fusion.1
  307.4 114.5 %all-reduce.14.cloned.1.call-done = (f32[512,768]{1,0:T(8,128)}, f32[512,768]{1,0:T(8,128)}) async-done(((f32[512,768]{1,0:T(8,128)}, f32[512,768]{1,0:T(8,128)}), (f32[512,768]{1,0:T(8,128)}, f32[512,768]{1,0:T(8,128)})) %all-reduce.14.cloned.1.call-update) | async-done | bytes 3145744 | tf_op jit(solution)/shard_map/psum | solution.py:207
  421.9 3.6 multiply_reduce_fusion.6
  426.7 66.1 %all-reduce.18.cloned.1.call-done = (bf16[512,768]{1,0:T(8,128)(2,1)}, bf16[512,768]{1,0:T(8,128)(2,1)}) async-done(((bf16[512,768]{1,0:T(8,128)(2,1)}, bf16[512,768]{1,0:T(8,128)(2,1)}), (bf16[512,768]{1,0:T(8,128)(2,1)}, bf16[512,768]{1,0:T(8,128)(2,1)})) %all-reduce.18.cloned.1.call-update) | async-done | bytes 1572880 | tf_op jit(solution)/shard_map/psum | solution.py:120
  492.8 5.0 fusion.183
  564.9 6.8 reduce-scatter.24.cloned.1.call-done
  576.7 14.7 %reduce-scatter.28.cloned.1.call-done = f32[512,192]{0,1:T(8,128)} async-done(((f32[1024,192]{0,1:T(8,128)}), f32[512,192]{0,1:T(8,128)}) %reduce-scatter.28.cloned.1.call-update) | async-done | bytes 393232 | tf_op jit(solution)/shard_map/reduce_scatter | solution.py:266
  593.1 3.3 convolution_bitcast_fusion
  614.2 4.3 copy.85
  618.5 4.7 reshape.318
  623.6 4.1 fusion.66
  630.0 88.1 %all-reduce.12.cloned.1.call-done = (f32[512,768]{1,0:T(8,128)}, f32[512,768]{1,0:T(8,128)}) async-done(((f32[512,768]{1,0:T(8,128)}, f32[512,768]{1,0:T(8,128)}), (f32[512,768]{1,0:T(8,128)}, f32[512,768]{1,0:T(8,128)})) %all-reduce.12.cloned.1.call-update) | async-done | bytes 3145744 | tf_op jit(solution)/shard_map/psum | solution.py:277
  730.0 4.9 convolution_add_fusion
  752.1 24.1 %all-reduce.2 = (f32[2,3,64]{2,1,0:T(4,128)S(1)}, f32[12,64]{1,0:T(8,128)S(1)}) all-reduce(f32[2,3,64]{2,1,0:T(4,128)S(1)} %maximum_add_fusion.3, f32[12,64]{1,0:T(8,128)} %add.400), channel_id=9, replica_groups=mesh['dp'=4,'seq'=2,'tensor'=4] {'dp','seq'}, use_global_device_ids=true, to_apply=%region_49.50.clone | all-reduce | flops 1152 | bytes 9216
  780.9 3.7 fusion.56
  787.3 9.6 %reduce-scatter.42.cloned.1.call-done = f32[96,2]{1,0:T(8,128)} async-done(((f32[768,2]{1,0:T(8,128)}), f32[96,2]{1,0:T(8,128)}) %reduce-scatter.42.cloned.1.call-update) | async-done | bytes 784
  798.4 45.2 %reduce-scatter.34.cloned.1.call-done = f32[768,96]{0,1:T(8,128)} async-done(((f32[768,768]{0,1:T(8,128)}), f32[768,96]{0,1:T(8,128)}) %reduce-scatter.34.cloned.1.call-update) | async-done | bytes 294928 | tf_op jit(solution)/shard_map/reduce_scatter | solution.py:297
  843.6 46.1 %reduce-scatter.32.cloned.1.call-done = f32[96,768]{1,0:T(8,128)} async-done(((f32[768,768]{1,0:T(8,128)}), f32[96,768]{1,0:T(8,128)}) %reduce-scatter.32.cloned.1.call-update) | async-done | bytes 294928 | tf_op jit(solution)/shard_map/reduce_scatter | solution.py:295
  (500 shorter events, 191.1 us)
Async XLA Ops:
  8.0 27.0 %copy-start = (bf16[2,512,768]{2,1,0:T(8,128)(2,1)S(1)}, bf16[2,512,768]{2,1,0:T(8,128)(2,1)}, u32[]{:S(2)}) copy-start(bf16[2,512,768]{2,1,0:T(8,128)(2,1)} %param.12) | copy-start | bytes 4718596
  8.0 271.5 %all-reduce.16.cloned.1.call-start = ((), (), s32[]{:S(2)}) async-start(), calls=%async_computation.26 | async-start | bytes 6291456 | tf_op jit(solution)/shard_map/psum | solution.py:111
  33.3 15.8 %copy-start.75 = (bf16[3,96,192]{2,1,0:T(8,128)(2,1)S(1)}, bf16[3,96,192]{2,1,0:T(8,128)(2,1)}, u32[]{:S(2)}) copy-start(bf16[3,96,192]{2,1,0:T(8,128)(2,1)} %param.14) | copy-start | bytes 331780
  35.0 40.7 %copy-start.90 = (f32[512]{0:T(512)}, f32[512]{0:T(512)S(1)}, u32[]{:S(2)}) copy-start(f32[512]{0:T(512)S(1)} %get-tuple-element.168) | copy-start | bytes 6148
  35.0 42.9 %copy-start.92 = (f32[512]{0:T(512)}, f32[512]{0:T(512)S(1)}, u32[]{:S(2)}) copy-start(f32[512]{0:T(512)S(1)} %get-tuple-element.169) | copy-start | bytes 6148
  35.6 39.5 %copy-start.110 = (f32[512]{0:T(512)}, f32[512]{0:T(512)S(1)}, u32[]{:S(2)}) copy-start(f32[512]{0:T(512)S(1)} %get-tuple-element.87) | copy-start | bytes 6148
  36.2 41.6 %copy-start.105 = (f32[512]{0:T(512)}, f32[512]{0:T(512)S(1)}, u32[]{:S(2)}) copy-start(f32[512]{0:T(512)S(1)} %fusion.151) | copy-start | bytes 6148
  36.2 39.5 %copy-start.107 = (f32[512]{0:T(512)}, f32[512]{0:T(512)S(1)}, u32[]{:S(2)}) copy-start(f32[512]{0:T(512)S(1)} %fusion.153) | copy-start | bytes 6148
  90.3 17.6 %copy-start.64 = (bf16[512,192]{0,1:T(8,128)(2,1)}, bf16[512,192]{0,1:T(8,128)(2,1)S(1)}, u32[]{:S(2)}) copy-start(bf16[512,192]{0,1:T(8,128)(2,1)S(1)} %get-tuple-element.126) | copy-start | bytes 589828
  108.0 17.8 %copy-start.63 = (bf16[512,192]{0,1:T(8,128)(2,1)S(1)}, bf16[512,192]{0,1:T(8,128)(2,1)}, u32[]{:S(2)}) copy-start(bf16[512,192]{0,1:T(8,128)(2,1)} %get-tuple-element.127) | copy-start | bytes 589828
  108.0 26.1 %copy-start.62 = (bf16[512,192]{0,1:T(8,128)(2,1)S(1)}, bf16[512,192]{0,1:T(8,128)(2,1)}, u32[]{:S(2)}) copy-start(bf16[512,192]{0,1:T(8,128)(2,1)} %get-tuple-element.138) | copy-start | bytes 589828
  125.8 18.4 %copy-start.14 = (f32[512,1024]{1,0:T(8,128)S(1)}, f32[512,1024]{1,0:T(8,128)}, u32[]{:S(2)}) copy-start(f32[512,1024]{1,0:T(8,128)} %get-tuple-element.149) | copy-start | bytes 6291460
  134.0 20.0 %copy-start.38 = (bf16[1024,192]{0,1:T(8,128)(2,1)}, bf16[1024,192]{0,1:T(8,128)(2,1)S(1)}, u32[]{:S(2)}) copy-start(bf16[1024,192]{0,1:T(8,128)(2,1)S(1)} %all_gather.74) | copy-start | bytes 1179652
  157.8 126.5 %all-gather.8.cloned.1.call-start = ((), (), s32[]{:S(2)}) async-start(), calls=%async_computation.11 | async-start | bytes 1327104 | tf_op jit(solution)/shard_map/all_gather | solution.py:61
  158.3 132.0 %all-gather.10.cloned.1.call-start = ((), (), s32[]{:S(2)}) async-start(), calls=%async_computation.12 | async-start | bytes 1327104 | tf_op jit(solution)/shard_map/all_gather | solution.py:63
  158.9 262.9 %all-reduce.14.cloned.1.call-start = ((), (), s32[]{:S(2)}) async-start(), calls=%async_computation.25 | async-start | bytes 6291456 | tf_op jit(solution)/shard_map/psum | solution.py:207
  281.9 140.0 %copy-start.19 = (f32[512,768]{1,0:T(8,128)}, f32[512,768]{1,0:T(8,128)S(1)}, u32[]{:S(2)}) copy-start(f32[512,768]{1,0:T(8,128)S(1)} %get-tuple-element.121) | copy-start | bytes 4718596
  281.9 210.9 %copy-start.97 = (f32[512]{0:T(512)}, f32[512]{0:T(512)S(1)}, u32[]{:S(2)}) copy-start(f32[512]{0:T(512)S(1)} %broadcast_multiply_fusion) | copy-start | bytes 6148
  301.3 191.6 %all-reduce.18.cloned.1.call-start = ((), (), s32[]{:S(2)}) async-start(), calls=%async_computation.27 | async-start | bytes 3145728 | tf_op jit(solution)/shard_map/psum | solution.py:120
  307.2 254.3 %reduce-scatter.26.cloned.1.call-start = ((), (), s32[]{:S(2)}) async-start(), calls=%async_computation.14 | async-start | bytes 1179648 | tf_op jit(solution)/shard_map/reduce_scatter | solution.py:267
  515.8 47.4 %reduce-scatter.30.cloned.1.call-start = ((), (), s32[]{:S(2)}) async-start(), calls=%async_computation.16 | async-start | bytes 1179648 | tf_op jit(solution)/shard_map/reduce_scatter | solution.py:267
  530.2 41.5 %reduce-scatter.24.cloned.1.call-start = ((), (), s32[]{:S(2)}) async-start(), calls=%async_computation.13 | async-start | bytes 1179648 | tf_op jit(solution)/shard_map/reduce_scatter | solution.py:266
  542.5 48.8 %reduce-scatter.28.cloned.1.call-start = ((), (), s32[]{:S(2)}) async-start(), calls=%async_computation.15 | async-start | bytes 1179648 | tf_op jit(solution)/shard_map/reduce_scatter | solution.py:266
  557.4 160.6 %all-reduce.12.cloned.1.call-start = ((), (), s32[]{:S(2)}) async-start(), calls=%async_computation.24 | async-start | bytes 6291456 | tf_op jit(solution)/shard_map/psum | solution.py:277
  596.4 149.9 %reduce-scatter.44.cloned.1.call-start = ((), (), s32[]{:S(2)}) async-start(), calls=%async_computation.23 | async-start | bytes 442368
  605.0 142.7 %reduce-scatter.38.cloned.1.call-start = ((), (), s32[]{:S(2)}) async-start(), calls=%async_computation.20 | async-start | bytes 884736
  610.0 167.6 %reduce-scatter.36.cloned.1.call-start = ((), (), s32[]{:S(2)}) async-start(), calls=%async_computation.19 | async-start | bytes 2211840
  623.2 162.7 %reduce-scatter.40.cloned.1.call-start = ((), (), s32[]{:S(2)}) async-start(), calls=%async_computation.21 | async-start | bytes 442368
  726.9 70.1 %reduce-scatter.42.cloned.1.call-start = ((), (), s32[]{:S(2)}) async-start(), calls=%async_computation.22 | async-start | bytes 442368
  729.9 113.7 %reduce-scatter.34.cloned.1.call-start = ((), (), s32[]{:S(2)}) async-start(), calls=%async_computation.18 | async-start | bytes 2654208 | tf_op jit(solution)/shard_map/reduce_scatter | solution.py:297
  734.9 154.9 %reduce-scatter.32.cloned.1.call-start = ((), (), s32[]{:S(2)}) async-start(), calls=%async_computation.17 | async-start | bytes 2654208 | tf_op jit(solution)/shard_map/reduce_scatter | solution.py:295
  746.3 34.7 %copy-start.94 = (f32[512]{0:T(512)S(1)}, f32[512]{0:T(512)}, u32[]{:S(2)}) copy-start(f32[512]{0:T(512)} %copy-done.92) | copy-start | bytes 6148
  (124 other events, 387.1 us)
Sparse Core Ops, SparseCore 0:
  157.9 121.6 all-reduce.15
  301.4 120.4 all-reduce.13
  424.3 68.4 all-reduce.17
  596.5 121.4 all-reduce.11
Sparse Core Ops, SparseCore 1:
  160.1 24.0 all-gather.7
  186.0 23.9 all-gather.9
  515.9 16.4 reduce-scatter.25
  534.6 17.3 reduce-scatter.29
  554.3 17.4 reduce-scatter.23
  574.1 17.2 reduce-scatter.27
  605.1 34.0 reduce-scatter.43
  642.2 34.9 reduce-scatter.37
  680.5 40.1 reduce-scatter.35
  727.0 32.8 reduce-scatter.39
  763.1 33.8 reduce-scatter.41
  801.3 42.3 reduce-scatter.33
  847.4 42.3 reduce-scatter.31
where the time goes:
time: 906 us; the launch traced here: 898 us
  waiting for transfers between devices  484 us (53%)
  blocking collectives  160 us (18%)
  matrix products  111 us (12%)
  other arithmetic  67.5 us (7%)
  local copies, waits for them, and re-layouts  55.2 us (6%)
  between operations  18.2 us (2%)
    psum x1, waiting for transfers between devices, per_device(): lax.psum(jnp.einsum('cf,df->cd', grad_pre, upward_full, preferred_element...  114 us
    psum x1, waiting for transfers between devices, per_device(): lax.psum(jnp.dot(attended, mixer_weights, preferred_element_type=jnp.floa...  91.1 us
    psum x1, waiting for transfers between devices, per_device(): lax.psum(jnp.einsum('tce,tde->cd', triple, entry_weights, preferred_eleme...  88.1 us
    psum x1, waiting for transfers between devices, per_device(): lax.psum(jnp.dot(activated, downward_full, preferred_element_type=jnp.flo...  66.1 us
    reduce_scatter x1, waiting for transfers between devices, per_device(): lax.psum_scatter(upward_acc, ('dp', 'seq'), scatter_dimension=0, tiled=True)  46.1 us
    unnamed x298, local copies, waits for them, and re-layouts  46 us
    reduce_scatter x1, waiting for transfers between devices, per_device(): lax.psum_scatter(downward_acc, ('dp', 'seq'), scatter_dimension=1, tiled=...  45.2 us
    unnamed x1, blocking collectives  24.1 us
  transfers between devices with their start and end apart: 17, of which 9 were waited for; matrix products, arithmetic and copies ran while one was open for 17% of the time, Pallas kernels for 0%

commit v1 on v0

v1 whole, which is shorter than its diff:
```python
import functools

import jax
import jax.numpy as jnp
from jax import lax
from jax.experimental import pallas as pl
from jax.experimental.pallas import tpu as pltpu
from jax.sharding import PartitionSpec as P

LANES = 128
SHARDS = ("dp", "seq")


def norm_stats(values):
    average = jnp.mean(values, axis=-1, keepdims=True)
    centered = values - average
    inverse = lax.rsqrt(jnp.mean(centered * centered, axis=-1, keepdims=True) + 1e-05)
    return centered * inverse, inverse


def norm_back(normal, inverse, gain_row, grad):
    scaled = grad * gain_row
    return inverse * (
        scaled
        - jnp.mean(scaled, axis=-1, keepdims=True)
        - normal * jnp.mean(scaled * normal, axis=-1, keepdims=True)
    )


def gelu_tanh(values):
    return (
        0.5
        * values
        * (1.0 + jnp.tanh(0.7978845608028654 * (values + 0.044715 * values * values * values)))
    )


def head_scores(query_head, key_head, allowed):
    scores = (
        jnp.einsum("qe,ke->qk", query_head, key_head, preferred_element_type=jnp.float32) * 0.125
    )
    return jnp.where(allowed, scores, -1e30)


def dot(equation, left, right):
    return jnp.einsum(equation, left, right, preferred_element_type=jnp.float32)


def line_sum_kernel(count, x_ref, out_ref, from_left, from_right, to_right, to_left, held, sems):
    me = lax.axis_index("tensor")
    streams = x_ref.shape[0]
    last = count - 1

    def neighbour(step):
        return {"tensor": jnp.clip(me + step, 0, last)}

    def copy(source, target, kind, stream, chunk, step):
        return pltpu.make_async_remote_copy(
            src_ref=source,
            dst_ref=target,
            send_sem=sems.at[2 * kind, stream, chunk],
            recv_sem=sems.at[2 * kind + 1, stream, chunk],
            device_id=neighbour(step),
            device_id_type=pl.DeviceIdType.MESH,
        )

    def partial(stream, owner, step, mine):
        arrived, leaving = (from_left, to_right) if step > 0 else (from_right, to_left)
        source = x_ref.at[stream, owner] if mine else leaving.at[stream, owner]
        return copy(source, arrived.at[stream, owner], 0 if step > 0 else 1, stream, owner, step)

    def total(stream, owner, step):
        place = held.at[stream, owner]
        return copy(place, place, 2 if step > 0 else 3, stream, owner, step)

    def send_partials(stream):
        for k in range(last):
            for step in (1, -1):
                owner = last - k if step > 0 else k
                arrived, leaving = (from_left, to_right) if step > 0 else (from_right, to_left)
                first = me == 0 if step > 0 else me == last
                inside = (me > 0) & (me < owner) if step > 0 else (me < last) & (me > owner)

                @pl.when(first)
                def _():
                    partial(stream, owner, step, True).start()

                @pl.when(inside)
                def _():
                    partial(stream, owner, step, False).wait_recv()
                    leaving[stream, owner] = (
                        arrived[stream, owner].astype(jnp.float32)
                        + x_ref[stream, owner].astype(jnp.float32)
                    ).astype(jnp.bfloat16)
                    partial(stream, owner, step, False).start()

    def finish(stream):
        own = x_ref[stream, pl.ds(me, 1)].astype(jnp.float32)

        @pl.when(me == 0)
        def _():
            partial(stream, me, -1, False).wait_recv()
            right = from_right[stream, pl.ds(me, 1)].astype(jnp.float32)
            held[stream, pl.ds(me, 1)] = (own + right).astype(jnp.bfloat16)

        @pl.when(me == last)
        def _():
            partial(stream, me, 1, False).wait_recv()
            left = from_left[stream, pl.ds(me, 1)].astype(jnp.float32)
            held[stream, pl.ds(me, 1)] = (own + left).astype(jnp.bfloat16)

        @pl.when((me > 0) & (me < last))
        def _():
            partial(stream, me, -1, False).wait_recv()
            partial(stream, me, 1, False).wait_recv()
            left = from_left[stream, pl.ds(me, 1)].astype(jnp.float32)
            right = from_right[stream, pl.ds(me, 1)].astype(jnp.float32)
            held[stream, pl.ds(me, 1)] = (own + left + right).astype(jnp.bfloat16)

        @pl.when(me < last)
        def _():
            total(stream, me, 1).start()

        @pl.when(me > 0)
        def _():
            total(stream, me, -1).start()

    def forward(stream):
        for k in range(1, count):
            for step in (1, -1):
                chunk = me - k if step > 0 else me + k
                comes = chunk >= 0 if step > 0 else chunk <= last
                goes = comes & (me < last) if step > 0 else comes & (me > 0)

                @pl.when(comes)
                def _():
                    total(stream, chunk, step).wait_recv()

                if k < last:

                    @pl.when(goes)
                    def _():
                        total(stream, chunk, step).start()

    barrier = pltpu.get_barrier_semaphore()
    for step in (1, -1):

        @pl.when(me < last if step > 0 else me > 0)
        def _():
            pl.semaphore_signal(
                barrier, inc=1, device_id=neighbour(step), device_id_type=pl.DeviceIdType.MESH
            )

    peers = jnp.where(me < last, 1, 0) + jnp.where(me > 0, 1, 0)
    pl.semaphore_wait(barrier, peers)

    for tick in range(streams + 2):
        if tick < streams:
            send_partials(tick)
        if 0 <= tick - 1 < streams:
            finish(tick - 1)
        if 0 <= tick - 2:
            forward(tick - 2)
            out_ref[tick - 2] = held[tick - 2]
    for stream in range(streams):
        for k in range(last):
            for step in (1, -1):
                owner = last - k if step > 0 else k

                @pl.when(me < owner if step > 0 else me > owner)
                def _():
                    partial(stream, owner, step, False).wait_send()

                chunk = me - k if step > 0 else me + k
                goes = (chunk >= 0) & (me < last) if step > 0 else (chunk <= last) & (me > 0)

                @pl.when(goes)
                def _():
                    total(stream, chunk, step).wait_send()


def tensor_sum(parts, streams, ident):
    count = lax.axis_size("tensor")
    values = jnp.concatenate([part.astype(jnp.bfloat16) for part in parts], axis=0)
    rows, width = values.shape
    shape = (streams, count, rows // (streams * count), width)
    scratch = [pltpu.VMEM(shape, jnp.bfloat16)] * 5
    summed = pl.pallas_call(
        functools.partial(line_sum_kernel, count),
        out_shape=jax.ShapeDtypeStruct(shape, jnp.bfloat16),
        in_specs=[pl.BlockSpec(memory_space=pltpu.VMEM)],
        out_specs=pl.BlockSpec(memory_space=pltpu.VMEM),
        scratch_shapes=scratch + [pltpu.SemaphoreType.DMA((8, streams, count))],
        compiler_params=pltpu.CompilerParams(collective_id=ident, has_side_effects=True),
        name="line_sum",
    )(values.reshape(shape))
    return jnp.split(summed.reshape(rows, width), len(parts), axis=0)


def pack_small(small, rows):
    columns = -(-small.shape[-1] // rows)
    padded = -(-columns // LANES) * LANES
    lead = small.shape[:-1]
    pads = [(0, 0)] * len(lead)
    filled = jnp.pad(small, pads + [(0, rows * columns - small.shape[-1])])
    filled = filled.reshape(lead + (rows, columns))
    return jnp.pad(filled, pads + [(0, 0), (0, padded - columns)])


def unpack_small(block, rows, size):
    columns = -(-size // rows)
    return block[:, :columns].reshape(-1, rows * columns)[:, :size]


def per_device(
    tokens,
    segments,
    projections,
    offsets,
    mixing,
    upward,
    thresholds,
    downward,
    scales,
    shifts,
    biases,
    cotangent,
):
    micro, block_len, width = tokens.shape
    seq_len = segments.shape[1]
    shards = lax.axis_size(SHARDS)
    heads = offsets.shape[1]
    piece = offsets.shape[2]
    head_size = piece * shards
    inner = heads * head_size
    rows = upward.shape[0]
    hidden_units = upward.shape[1]
    start = lax.axis_index("seq") * block_len
    query_pos = start + jnp.arange(block_len, dtype=jnp.int32)
    key_pos = jnp.arange(seq_len, dtype=jnp.int32)

    small = jnp.concatenate(
        [
            offsets.reshape(-1),
            thresholds.reshape(-1),
            scales.reshape(-1),
            shifts.reshape(-1),
            biases.reshape(-1),
        ]
    )
    small_size = small.shape[0]
    packed = jnp.concatenate(
        [
            upward,
            downward.T,
            mixing.T,
            projections[0],
            projections[1],
            projections[2],
            pack_small(small, rows),
        ],
        axis=1,
    )
    full = lax.all_gather(packed, SHARDS, axis=0, tiled=True)
    up = full[:, :hidden_units]
    down_t = full[:, hidden_units : 2 * hidden_units]
    mix_t = full[:, 2 * hidden_units : 2 * hidden_units + inner]
    entry = full[:, 2 * hidden_units + inner : 2 * hidden_units + 4 * inner]
    table = unpack_small(full[:, 2 * hidden_units + 4 * inner :], rows, small_size)
    table = table.astype(jnp.float32)
    cuts = [0, offsets.size, offsets.size + thresholds.size]
    offset_rows = (
        table[:, cuts[0] : cuts[1]]
        .reshape(shards, 2, heads, piece)
        .transpose(1, 2, 0, 3)
        .reshape(2, inner)
    )
    threshold_row = (
        table[:, cuts[1] : cuts[2]]
        .reshape(shards, thresholds.shape[0], thresholds.shape[1])
        .transpose(1, 0, 2)
        .reshape(-1)
    )
    norm_rows = (
        table[:, cuts[2] :].reshape(shards, 6, rows).transpose(1, 0, 2).reshape(6, shards * rows)
    )
    scale_rows, shift_rows, bias_rows = norm_rows[0:2], norm_rows[2:4], norm_rows[4:6]

    inputs = []
    normals = []
    inverses = []
    normed = []
    stacks = []
    for b in range(micro):
        value = tokens[b].astype(jnp.float32)
        normal, inverse = norm_stats(value)
        inputs.append(value)
        normals.append(normal)
        inverses.append(inverse)
        normed.append((normal * scale_rows[0] + shift_rows[0]).astype(jnp.bfloat16))
        stacks.append(dot("cd,de->ce", normed[b], entry))
    query_b = [(s[:, :inner] + offset_rows[0]).astype(jnp.bfloat16) for s in stacks]
    key_value = jnp.stack(
        [
            jnp.concatenate(
                [s[:, inner : 2 * inner], s[:, 2 * inner :] + offset_rows[1]], axis=1
            ).astype(jnp.bfloat16)
            for s in stacks
        ]
    )
    key_value_full = lax.all_gather(key_value, "seq", axis=1, tiled=True)

    allowed = []
    probs_all = []
    attended = []
    branch = []
    for b in range(micro):
        seg_row = segments[b]
        own_seg = lax.dynamic_slice_in_dim(seg_row, start, block_len)
        allowed.append(
            (key_pos[None, :] <= query_pos[:, None]) & (seg_row[None, :] == own_seg[:, None])
        )
        pieces = []
        totals = []
        for h in range(heads):
            cols = slice(h * head_size, (h + 1) * head_size)
            vcols = slice(inner + h * head_size, inner + (h + 1) * head_size)
            scores = head_scores(query_b[b][:, cols], key_value_full[b][:, cols], allowed[b])
            log_total = jax.nn.logsumexp(scores, axis=1, keepdims=True)
            weights_b = jnp.exp(scores - log_total).astype(jnp.bfloat16)
            pieces.append(dot("qk,ke->qe", weights_b, key_value_full[b][:, vcols]))
            totals.append(log_total)
        probs_all.append(totals)
        attended.append(jnp.concatenate(pieces, axis=1).astype(jnp.bfloat16))
        branch.append(dot("ce,de->cd", attended[b], mix_t))

    branch = tensor_sum(branch, 4, 0)
    hidden = []
    normals2 = []
    inverses2 = []
    normed2 = []
    pre_act = []
    activated = []
    lifted = []
    for b in range(micro):
        hidden.append(inputs[b] + branch[b].astype(jnp.float32) + bias_rows[0])
        normal, inverse = norm_stats(hidden[b])
        normals2.append(normal)
        inverses2.append(inverse)
        normed2.append((normal * scale_rows[1] + shift_rows[1]).astype(jnp.bfloat16))
        pre_act.append(dot("cd,df->cf", normed2[b], up) + threshold_row)
        activated.append(gelu_tanh(pre_act[b]).astype(jnp.bfloat16))

    grad_pre = []
    grad_sum2 = []
    for b in range(micro):
        grad_act = dot("cd,df->cf", cotangent[b], down_t)
        unused, gelu_back = jax.vjp(gelu_tanh, pre_act[b])
        grad_pre.append(gelu_back(grad_act)[0].astype(jnp.bfloat16))
        grad_sum2.append(dot("cf,df->cd", grad_pre[b], up))
    for b in range(micro):
        lifted.append(dot("cf,df->cd", activated[b], down_t))
    sums = tensor_sum(grad_sum2 + lifted, 4, 1)
    grad_sum2, lifted = sums[:micro], sums[micro:]
    results = [
        (hidden[b] + lifted[b].astype(jnp.float32) + bias_rows[1]).astype(jnp.bfloat16)
        for b in range(micro)
    ]

    both = lambda parts: jnp.concatenate(parts, axis=0)
    grad_pre_all = both(grad_pre)
    cotangent_all = cotangent.reshape(micro * block_len, width)
    threshold_grad = jnp.sum(grad_pre_all.astype(jnp.float32), axis=0)
    ffn_grads = jnp.concatenate(
        [
            dot("cd,cf->df", both(normed2), grad_pre_all).astype(jnp.bfloat16),
            dot("cd,cf->df", cotangent_all, both(activated)).astype(jnp.bfloat16),
        ],
        axis=1,
    )
    ffn_own = lax.psum_scatter(ffn_grads, SHARDS, scatter_dimension=0, tiled=True)

    grad_hidden = []
    grad_hidden_b = []
    scale2 = 0.0
    shift2 = 0.0
    query_grads = []
    key_value_grads = []
    for b in range(micro):
        grad_norm2 = grad_sum2[b].astype(jnp.float32)
        grad_hidden.append(
            cotangent[b].astype(jnp.float32)
            + norm_back(normals2[b], inverses2[b], scale_rows[1], grad_norm2)
        )
        scale2 += jnp.sum(grad_norm2 * normals2[b], axis=0)
        shift2 += jnp.sum(grad_norm2, axis=0)
        grad_hidden_b.append(grad_hidden[b].astype(jnp.bfloat16))
        grad_attended = dot("cd,de->ce", grad_hidden_b[b], mix_t).astype(jnp.bfloat16)
        grads_q = []
        grads_k = []
        grads_v = []
        for h in range(heads):
            cols = slice(h * head_size, (h + 1) * head_size)
            vcols = slice(inner + h * head_size, inner + (h + 1) * head_size)
            scores = head_scores(query_b[b][:, cols], key_value_full[b][:, cols], allowed[b])
            probs = jnp.exp(scores - probs_all[b][h])
            grad_slice = grad_attended[:, cols]
            grad_probs = dot("qe,ke->qk", grad_slice, key_value_full[b][:, vcols])
            delta = jnp.sum(probs * grad_probs, axis=1, keepdims=True)
            grad_scores = (probs * (grad_probs - delta)).astype(jnp.bfloat16)
            grads_q.append(dot("qk,ke->qe", grad_scores, key_value_full[b][:, cols]) * 0.125)
            grads_v.append(dot("qk,qe->ke", probs.astype(jnp.bfloat16), grad_slice))
            grads_k.append(dot("qk,qe->ke", grad_scores, query_b[b][:, cols]) * 0.125)
        query_grads.append(jnp.concatenate(grads_q, axis=1).astype(jnp.bfloat16))
        key_value_grads.append(jnp.concatenate(grads_k + grads_v, axis=1).astype(jnp.bfloat16))
    key_value_own = lax.psum_scatter(
        jnp.stack(key_value_grads), "seq", scatter_dimension=1, tiled=True
    )

    triples = []
    grad_normed = []
    for b in range(micro):
        triples.append(jnp.concatenate([query_grads[b], key_value_own[b]], axis=1))
        grad_normed.append(dot("ce,de->cd", triples[b], entry))
    grad_normed = tensor_sum(grad_normed, 4, 0)
    triple_all = both(triples)
    grad_hidden_all = both(grad_hidden_b)
    triple_sums = jnp.sum(triple_all.astype(jnp.float32), axis=0)
    scale1 = 0.0
    shift1 = 0.0
    bias1 = 0.0
    input_grads = []
    for b in range(micro):
        grad_norm = grad_normed[b].astype(jnp.float32)
        back = norm_back(normals[b], inverses[b], scale_rows[0], grad_norm)
        input_grads.append((grad_hidden[b] + back).astype(jnp.bfloat16))
        scale1 += jnp.sum(grad_norm * normals[b], axis=0)
        shift1 += jnp.sum(grad_norm, axis=0)
        bias1 += jnp.sum(grad_hidden[b], axis=0)
    bias2 = jnp.sum(cotangent_all.astype(jnp.float32), axis=0)

    offset_grad = jnp.stack([triple_sums[:inner], triple_sums[2 * inner :]])
    small_grads = jnp.concatenate(
        [
            offset_grad.reshape(2, heads, shards, piece).transpose(2, 0, 1, 3).reshape(shards, -1),
            threshold_grad.reshape(thresholds.shape[0], shards, thresholds.shape[1])
            .transpose(1, 0, 2)
            .reshape(shards, -1),
            jnp.stack([scale1, scale2, shift1, shift2, bias1, bias2])
            .reshape(6, shards, rows)
            .transpose(1, 0, 2)
            .reshape(shards, -1),
        ],
        axis=1,
    )
    small_block = pack_small(small_grads, rows).reshape(shards * rows, -1)
    att_grads = jnp.concatenate(
        [
            dot("cd,ce->de", grad_hidden_all, both(attended)).astype(jnp.bfloat16),
            dot("cd,ce->de", both(normed), triple_all).astype(jnp.bfloat16),
            small_block.astype(jnp.bfloat16),
        ],
        axis=1,
    )
    att_own = lax.psum_scatter(att_grads, SHARDS, scatter_dimension=0, tiled=True)
    att_own = att_own.astype(jnp.float32)
    ffn_own = ffn_own.astype(jnp.float32)
    own_small = unpack_small(att_own[:, 4 * inner :], rows, small_size)[0]
    own_norms = own_small[cuts[2] :].reshape(6, rows)
    own_entry = att_own[:, inner : 4 * inner]
    return (
        jnp.stack(results),
        jnp.stack(input_grads),
        jnp.stack([own_entry[:, t * inner : (t + 1) * inner] for t in range(3)]),
        own_small[cuts[0] : cuts[1]].reshape(offsets.shape),
        att_own[:, :inner].T,
        ffn_own[:, :hidden_units],
        own_small[cuts[1] : cuts[2]].reshape(thresholds.shape),
        ffn_own[:, hidden_units:].T,
        own_norms[0:2],
        own_norms[2:4],
        own_norms[4:6],
    )


def solution(mesh):
    placed = (
        P("dp", "seq", None),
        P("dp", None),
        P(None, ("dp", "seq"), "tensor"),
        P(None, "tensor", ("dp", "seq")),
        P("tensor", ("dp", "seq")),
        P(("dp", "seq"), "tensor"),
        P("tensor", ("dp", "seq")),
        P("tensor", ("dp", "seq")),
        P(None, ("dp", "seq")),
        P(None, ("dp", "seq")),
        P(None, ("dp", "seq")),
        P("dp", "seq", None),
    )
    return jax.shard_map(
        per_device,
        mesh=mesh,
        in_specs=placed,
        out_specs=(
            P("dp", "seq", None),
            P("dp", "seq", None),
            P(None, ("dp", "seq"), "tensor"),
            P(None, "tensor", ("dp", "seq")),
            P("tensor", ("dp", "seq")),
            P(("dp", "seq"), "tensor"),
            P("tensor", ("dp", "seq")),
            P("tensor", ("dp", "seq")),
            P(None, ("dp", "seq")),
            P(None, ("dp", "seq")),
            P(None, ("dp", "seq")),
        ),
        check_vma=False,
    )
```

time: 906 us -> 539 us (0.59)
  waiting for transfers between devices: 484 us -> 76.9 us
  Pallas kernels: 0 us -> 259 us
  blocking collectives: 160 us -> 0 us
  matrix products: 111 us -> 60.9 us
  other arithmetic: 67.5 us -> 51 us
  local copies, waits for them, and re-layouts: 55.2 us -> 68.7 us
    psum x4 -> x0, waiting for transfers between devices: 360 us -> none  [the longest x1 114 us: per_device(): lax.psum(jnp.einsum('cf,df->cd', grad_pre, upward_full, preferred_element...]
    pallas_call x0 -> x3, Pallas kernels: none -> 259 us  [tensor_sum(): pl.pallas_call(functools.partial(line_sum_kernel, count), out_shape=jax.S...]
    all_gather x11 -> x0, blocking collectives: 136 us -> none  [the longest x1 23.8 us: per_device(): lax.all_gather(projections, ('dp', 'seq'), axis=1, tiled=True)]
    reduce_scatter x6 -> x1, waiting for transfers between devices: 113 us -> 1.07 us  [per_device(): lax.psum_scatter(jnp.stack(key_value_grads), 'seq', scatter_dimension=1,...]
    all_gather x2, waiting for transfers between devices: 0.01 us -> 53.6 us  [the longest x1 36.6 us: per_device(): full = lax.all_gather(packed, SHARDS, axis=0, tiled=True)]
    dot_general x52 -> x50, matrix products: 96.5 us -> 56.3 us  [dot(): return jnp.einsum(equation, left, right, preferred_element_type=jnp.float32)]
    unnamed x1 -> x0, blocking collectives: 24.1 us -> none
    unnamed x298 -> x283, local copies, waits for them, and re-layouts: 46 us -> 29.1 us
  transfers between devices with their start and end apart: 17 -> 5, of which waited for: 9 -> 4; matrix products, arithmetic and copies ran while one was open for 17% -> 16% of each run, Pallas kernels for 0% -> 14%
where the time goes in v1:
time: 539 us; the launch traced here: 533 us
  Pallas kernels  259 us (48%)
  waiting for transfers between devices  76.9 us (14%)
  local copies, waits for them, and re-layouts  68.7 us (13%)
  matrix products  60.9 us (11%)
  other arithmetic  51 us (9%)
  between operations  16 us (3%)
    pallas_call x3, Pallas kernels, tensor_sum(): pl.pallas_call(functools.partial(line_sum_kernel, count), out_shape=jax.S...  259 us
    dot_general x50, matrix products, dot(): return jnp.einsum(equation, left, right, preferred_element_type=jnp.float32)  56.3 us
    all_gather x1, waiting for transfers between devices, per_device(): full = lax.all_gather(packed, SHARDS, axis=0, tiled=True)  36.6 us
    unnamed x283, local copies, waits for them, and re-layouts  29.1 us
    unnamed x7, waiting for transfers between devices  22.3 us
    all_gather x1, waiting for transfers between devices, per_device(): key_value_full = lax.all_gather(key_value, 'seq', axis=1, tiled=True)  17 us
  transfers between devices with their start and end apart: 5, of which 4 were waited for; matrix products, arithmetic and copies ran while one was open for 16% of the time, Pallas kernels for 14%

profile of v1, /device:TPU:0, one launch (start us, length us, event | category | flops | bytes accessed | tf_op | source)
XLA Modules:
  0.0 532.9 jit_solution(7668447598777505340)
XLA Ops:
  13.2 1.9 concatenate.147
  16.1 36.6 %all-gather.3.cloned.1.call-done = bf16[768,2432]{1,0:T(8,128)(2,1)} async-done(((bf16[96,2432]{1,0:T(8,128)(2,1)}), bf16[768,2432]{1,0:T(8,128)(2,1)}) %all-gather.3.cloned.1.call-update) | async-done | bytes 3735568 | tf_op jit(solution)/shard_map/all_gather | solution.py:264
  56.4 2.9 fusion.175
  59.4 2.4 fusion.173
  68.3 1.9 slice_convert_fusion.7
  73.3 17.0 %all-gather.5.cloned.1.call-done = bf16[2,1024,384]{1,2,0:T(8,128)(2,1)} async-done(((bf16[2,512,384]{1,2,0:T(8,128)(2,1)}), bf16[2,1024,384]{1,2,0:T(8,128)(2,1)}) %all-gather.5.cloned.1.call-update) | async-done | bytes 1572880 | tf_op jit(solution)/shard_map/all_gather | solution.py:311
  107.3 76.7 %line_sum.3 = bf16[4,4,64,768]{3,2,1,0:T(8,128)(2,1)} custom-call(bf16[4,4,64,768]{3,2,1,0:T(8,128)(2,1)} %bitcast.335), custom_call_target="tpu_custom_call" | custom-call | tf_op jit(solution)/shard_map/line_sum/pallas_call | solution.py:188
  190.1 1.7 copy-done.46
  193.3 2.4 fusion.313
  196.7 2.4 fusion.314
  202.3 1.9 pad_maximum_fusion
  204.3 105.8 %line_sum.4 = bf16[4,4,128,768]{3,2,1,0:T(8,128)(2,1)} custom-call(bf16[4,4,128,768]{3,2,1,0:T(8,128)(2,1)} %bitcast.334), custom_call_target="tpu_custom_call" | custom-call | tf_op jit(solution)/shard_map/line_sum/pallas_call | solution.py:188
  310.1 4.9 convert_reduce_fusion.4
  315.2 2.7 fusion.301
  317.9 1.7 convolution_convert_fusion.9
  323.5 1.7 convolution_convert_fusion.8
  329.7 2.5 fusion.104
  342.6 3.4 fusion.96
  347.6 4.4 copy.79
  355.0 2.7 fusion.107
  376.0 2.6 convolution_convert_fusion.5
  378.6 2.5 convolution_convert_fusion.4
  382.3 76.4 %line_sum.5 = bf16[4,4,64,768]{3,2,1,0:T(8,128)(2,1)} custom-call(bf16[4,4,64,768]{3,2,1,0:T(8,128)(2,1)} %bitcast.336), custom_call_target="tpu_custom_call" | custom-call | tf_op jit(solution)/shard_map/line_sum/pallas_call | solution.py:188
  458.8 3.7 convert_reduce_fusion.2
  473.7 1.6 pad.21
  475.3 1.7 copy.70
  477.1 2.8 fusion.101
  481.1 2.5 copy.77
  484.0 1.8 slice_convert_fusion.3
  486.9 3.0 fusion.62
  490.0 1.8 fusion.48
  497.5 22.2 %reduce-scatter.10.cloned.1.call-done = bf16[96,896]{1,0:T(8,128)(2,1)} async-done(((bf16[768,896]{1,0:T(8,128)(2,1)}), bf16[96,896]{1,0:T(8,128)(2,1)}) %reduce-scatter.10.cloned.1.call-update) | async-done | bytes 172048
  (487 shorter events, 116.7 us)
Async XLA Ops:
  7.2 7.9 %copy-start = (bf16[2,512,768]{2,1,0:T(8,128)(2,1)S(1)}, bf16[2,512,768]{2,1,0:T(8,128)(2,1)}, u32[]{:S(2)}) copy-start(bf16[2,512,768]{2,1,0:T(8,128)(2,1)} %param.12) | copy-start | bytes 4718596
  7.2 45.5 %all-gather.3.cloned.1.call-start = ((), (), s32[]{:S(2)}) async-start(), calls=%async_computation.3 | async-start | bytes 4202496 | tf_op jit(solution)/shard_map/all_gather | solution.py:264
  15.1 75.2 %all-gather.5.cloned.1.call-start = ((), (), s32[]{:S(2)}) async-start(), calls=%async_computation.4 | async-start | bytes 2359296 | tf_op jit(solution)/shard_map/all_gather | solution.py:311
  15.4 49.7 %copy-start.87 = (f32[512]{0:T(512)}, f32[512]{0:T(512)S(1)}, u32[]{:S(2)}) copy-start(f32[512]{0:T(512)S(1)} %get-tuple-element.190) | copy-start | bytes 6148
  15.4 50.4 %copy-start.85 = (f32[512]{0:T(512)}, f32[512]{0:T(512)S(1)}, u32[]{:S(2)}) copy-start(f32[512]{0:T(512)S(1)} %get-tuple-element.189) | copy-start | bytes 6148
  16.1 48.4 %copy-start.96 = (f32[512]{0:T(512)}, f32[512]{0:T(512)S(1)}, u32[]{:S(2)}) copy-start(f32[512]{0:T(512)S(1)} %add_rsqrt_fusion.2) | copy-start | bytes 6148
  16.1 40.3 %copy-start.98 = (f32[512]{0:T(512)}, f32[512]{0:T(512)S(1)}, u32[]{:S(2)}) copy-start(f32[512]{0:T(512)S(1)} %add_rsqrt_fusion.3) | copy-start | bytes 6148
  62.9 303.7 %reduce-scatter.8.cloned.1.call-start = ((), (), s32[]{:S(2)}) async-start(), calls=%async_computation.5 | async-start | bytes 2359296 | tf_op jit(solution)/shard_map/reduce_scatter | solution.py:416
  91.7 7.5 %copy-start.38 = (bf16[1024,384]{0,1:T(8,128)(2,1)}, bf16[1024,384]{0,1:T(8,128)(2,1)S(1)}, u32[]{:S(2)}) copy-start(bf16[1024,384]{0,1:T(8,128)(2,1)S(1)} %get-tuple-element.126) | copy-start | bytes 2359300
  91.7 10.8 %copy-start.35 = (bf16[1024,384]{0,1:T(8,128)(2,1)}, bf16[1024,384]{0,1:T(8,128)(2,1)S(1)}, u32[]{:S(2)}) copy-start(bf16[1024,384]{0,1:T(8,128)(2,1)S(1)} %get-tuple-element.127) | copy-start | bytes 2359300
  94.9 5.5 %copy-start.8 = (f32[512,1024]{1,0:T(8,128)}, f32[512,1024]{1,0:T(8,128)S(1)}, u32[]{:S(2)}) copy-start(f32[512,1024]{1,0:T(8,128)S(1)} %get-tuple-element.162) | copy-start | bytes 6291460
  95.6 5.8 %copy-start.6 = (f32[512,1024]{1,0:T(8,128)}, f32[512,1024]{1,0:T(8,128)S(1)}, u32[]{:S(2)}) copy-start(f32[512,1024]{1,0:T(8,128)S(1)} %get-tuple-element.160) | copy-start | bytes 6291460
  96.4 6.2 %copy-start.4 = (f32[512,1024]{1,0:T(8,128)}, f32[512,1024]{1,0:T(8,128)S(1)}, u32[]{:S(2)}) copy-start(f32[512,1024]{1,0:T(8,128)S(1)} %get-tuple-element.158) | copy-start | bytes 6291460
  97.7 5.5 %copy-start.58 = (bf16[512,64]{0,1:T(8,128)(2,1)}, bf16[512,64]{0,1:T(8,128)(2,1)S(1)}, u32[]{:S(2)}) copy-start(bf16[512,64]{0,1:T(8,128)(2,1)S(1)} %convolution_convert_fusion.21) | copy-start | bytes 196612
  190.1 5.5 %copy-start.51 = (bf16[512,768]{1,0:T(8,128)(2,1)}, bf16[512,768]{1,0:T(8,128)(2,1)S(1)}, u32[]{:S(2)}) copy-start(bf16[512,768]{1,0:T(8,128)(2,1)S(1)} %get-tuple-element.117) | copy-start | bytes 2359300
  192.9 7.0 %copy-start.129 = (bf16[512,768]{1,0:T(8,128)(2,1)}, bf16[512,768]{1,0:T(8,128)(2,1)S(1)}, u32[]{:S(2)}) copy-start(bf16[512,768]{1,0:T(8,128)(2,1)S(1)} %get-tuple-element.171) | copy-start | bytes 2359300
  317.9 5.6 %copy-start.42 = (bf16[512,768]{1,0:T(8,128)(2,1)}, bf16[512,768]{1,0:T(8,128)(2,1)S(1)}, u32[]{:S(2)}) copy-start(bf16[512,768]{1,0:T(8,128)(2,1)S(1)} %get-tuple-element.109) | copy-start | bytes 2359300
  342.3 152.1 %reduce-scatter.12.cloned.1.call-start = ((), (), s32[]{:S(2)}) async-start(), calls=%async_computation.7 | async-start | bytes 2654208
  347.5 5.2 copy-start.110
  347.5 5.2 copy-start.111
  347.5 5.9 %copy-start.108 = (f32[768]{0:T(1024)S(1)}, f32[768]{0:T(1024)}, u32[]{:S(2)}) copy-start(f32[768]{0:T(1024)} %get-tuple-element.71) | copy-start | bytes 9220
  347.5 5.9 %copy-start.109 = (f32[768]{0:T(1024)S(1)}, f32[768]{0:T(1024)}, u32[]{:S(2)}) copy-start(f32[768]{0:T(1024)} %get-tuple-element.74) | copy-start | bytes 9220
  347.5 6.6 %copy-start.125 = (bf16[768]{0:T(1024)(128)(2,1)S(1)}, bf16[768]{0:T(1024)(128)(2,1)}, u32[]{:S(2)}) copy-start(bf16[768]{0:T(1024)(128)(2,1)} %get-tuple-element.185) | copy-start | bytes 4612
  347.5 6.6 %copy-start.126 = (bf16[768]{0:T(1024)(128)(2,1)S(1)}, bf16[768]{0:T(1024)(128)(2,1)}, u32[]{:S(2)}) copy-start(bf16[768]{0:T(1024)(128)(2,1)} %get-tuple-element.187) | copy-start | bytes 4612
  347.6 7.4 %copy-start.59 = (bf16[512,64]{0,1:T(8,128)(2,1)S(1)}, bf16[512,64]{0,1:T(8,128)(2,1)}, u32[]{:S(2)}) copy-start(bf16[512,64]{0,1:T(8,128)(2,1)} %copy-done.58) | copy-start | bytes 196612
  347.6 7.3 %copy-start.61 = (bf16[512,64]{0,1:T(8,128)(2,1)S(1)}, bf16[512,64]{0,1:T(8,128)(2,1)}, u32[]{:S(2)}) copy-start(bf16[512,64]{0,1:T(8,128)(2,1)} %copy-done.60) | copy-start | bytes 196612
  347.6 7.3 %copy-start.63 = (bf16[512,64]{0,1:T(8,128)(2,1)S(1)}, bf16[512,64]{0,1:T(8,128)(2,1)}, u32[]{:S(2)}) copy-start(bf16[512,64]{0,1:T(8,128)(2,1)} %copy-done.62) | copy-start | bytes 196612
  347.6 7.3 %copy-start.65 = (bf16[512,64]{0,1:T(8,128)(2,1)S(1)}, bf16[512,64]{0,1:T(8,128)(2,1)}, u32[]{:S(2)}) copy-start(bf16[512,64]{0,1:T(8,128)(2,1)} %copy-done.64) | copy-start | bytes 196612
  347.6 7.3 %copy-start.67 = (bf16[512,64]{0,1:T(8,128)(2,1)S(1)}, bf16[512,64]{0,1:T(8,128)(2,1)}, u32[]{:S(2)}) copy-start(bf16[512,64]{0,1:T(8,128)(2,1)} %copy-done.66) | copy-start | bytes 196612
  355.0 6.0 %copy-start.37 = (bf16[1024,384]{0,1:T(8,128)(2,1)S(1)}, bf16[1024,384]{0,1:T(8,128)(2,1)}, u32[]{:S(2)}) copy-start(bf16[1024,384]{0,1:T(8,128)(2,1)} %copy-done.35) | copy-start | bytes 2359300
  365.5 154.1 %reduce-scatter.10.cloned.1.call-start = ((), (), s32[]{:S(2)}) async-start(), calls=%async_computation.6 | async-start | bytes 1548288
  382.3 76.4 %copy-start.118 = (f32[2,4,64]{2,1,0:T(4,128)S(1)}, f32[2,4,64]{2,1,0:T(4,128)}, u32[]{:S(2)}) copy-start(f32[2,4,64]{2,1,0:T(4,128)} %rsqrt.54) | copy-start | bytes 6148
  (106 other events, 305.6 us)
Sparse Core Ops, SparseCore 0:
  15.2 37.4 all-gather.2
  63.0 27.1 all-gather.4
  342.4 24.1 reduce-scatter.7
  370.2 42.4 reduce-scatter.11
  484.0 35.5 reduce-scatter.9

commit v2 on v1

--- a/solution.py
+++ b/solution.py
@@ -73,26 +73,21 @@
         place = held.at[stream, owner]
         return copy(place, place, 2 if step > 0 else 3, stream, owner, step)
 
-    def send_partials(stream):
-        for k in range(last):
-            for step in (1, -1):
-                owner = last - k if step > 0 else k
-                arrived, leaving = (from_left, to_right) if step > 0 else (from_right, to_left)
-                first = me == 0 if step > 0 else me == last
-                inside = (me > 0) & (me < owner) if step > 0 else (me < last) & (me > owner)
-
-                @pl.when(first)
-                def _():
-                    partial(stream, owner, step, True).start()
-
-                @pl.when(inside)
-                def _():
-                    partial(stream, owner, step, False).wait_recv()
-                    leaving[stream, owner] = (
-                        arrived[stream, owner].astype(jnp.float32)
-                        + x_ref[stream, owner].astype(jnp.float32)
-                    ).astype(jnp.bfloat16)
-                    partial(stream, owner, step, False).start()
+    def send_partials(stream, hop):
+        for step in (1, -1):
+            arrived, leaving = (from_left, to_right) if step > 0 else (from_right, to_left)
+
+            @pl.when(me == hop if step > 0 else me == last - hop)
+            def _():
+                for k in range(last - hop):
+                    owner = last - k if step > 0 else k
+                    if hop > 0:
+                        partial(stream, owner, step, False).wait_recv()
+                        leaving[stream, owner] = (
+                            arrived[stream, owner].astype(jnp.float32)
+                            + x_ref[stream, owner].astype(jnp.float32)
+                        ).astype(jnp.bfloat16)
+                    partial(stream, owner, step, hop == 0).start()
 
     def finish(stream):
         own = x_ref[stream, pl.ds(me, 1)].astype(jnp.float32)
@@ -125,22 +120,21 @@
         def _():
             total(stream, me, -1).start()
 
-    def forward(stream):
-        for k in range(1, count):
-            for step in (1, -1):
-                chunk = me - k if step > 0 else me + k
-                comes = chunk >= 0 if step > 0 else chunk <= last
-                goes = comes & (me < last) if step > 0 else comes & (me > 0)
-
-                @pl.when(comes)
+    def forward(stream, k):
+        for step in (1, -1):
+            chunk = me - k if step > 0 else me + k
+            comes = chunk >= 0 if step > 0 else chunk <= last
+            goes = comes & (me < last) if step > 0 else comes & (me > 0)
+
+            @pl.when(comes)
+            def _():
+                total(stream, chunk, step).wait_recv()
+
+            if k < last:
+
+                @pl.when(goes)
                 def _():
-                    total(stream, chunk, step).wait_recv()
-
-                if k < last:
-
-                    @pl.when(goes)
-                    def _():
-                        total(stream, chunk, step).start()
+                    total(stream, chunk, step).start()
 
     barrier = pltpu.get_barrier_semaphore()
     for step in (1, -1):
@@ -154,14 +148,17 @@
     peers = jnp.where(me < last, 1, 0) + jnp.where(me > 0, 1, 0)
     pl.semaphore_wait(barrier, peers)
 
-    for tick in range(streams + 2):
-        if tick < streams:
-            send_partials(tick)
-        if 0 <= tick - 1 < streams:
-            finish(tick - 1)
-        if 0 <= tick - 2:
-            forward(tick - 2)
-            out_ref[tick - 2] = held[tick - 2]
+    for tick in range(streams + 2 * last):
+        for hop in range(last):
+            if 0 <= tick - hop < streams:
+                send_partials(tick - hop, hop)
+        if 0 <= tick - last < streams:
+            finish(tick - last)
+        for k in range(1, count):
+            if 0 <= tick - last - k < streams:
+                forward(tick - last - k, k)
+        if 0 <= tick - 2 * last < streams:
+            out_ref[tick - 2 * last] = held[tick - 2 * last]
     for stream in range(streams):
         for k in range(last):
             for step in (1, -1):
@@ -251,8 +248,6 @@
     small_size = small.shape[0]
     packed = jnp.concatenate(
         [
-            upward,
-            downward.T,
             mixing.T,
             projections[0],
             projections[1],
@@ -262,11 +257,9 @@
         axis=1,
     )
     full = lax.all_gather(packed, SHARDS, axis=0, tiled=True)
-    up = full[:, :hidden_units]
-    down_t = full[:, hidden_units : 2 * hidden_units]
-    mix_t = full[:, 2 * hidden_units : 2 * hidden_units + inner]
-    entry = full[:, 2 * hidden_units + inner : 2 * hidden_units + 4 * inner]
-    table = unpack_small(full[:, 2 * hidden_units + 4 * inner :], rows, small_size)
+    mix_t = full[:, :inner]
+    entry = full[:, inner : 4 * inner]
+    table = unpack_small(full[:, 4 * inner :], rows, small_size)
     table = table.astype(jnp.float32)
     cuts = [0, offsets.size, offsets.size + thresholds.size]
     offset_rows = (
@@ -309,6 +302,11 @@
         ]
     )
     key_value_full = lax.all_gather(key_value, "seq", axis=1, tiled=True)
+    packed_ffn = jnp.concatenate([upward, downward.T], axis=1)
+    packed_ffn, key_value_full = lax.optimization_barrier((packed_ffn, key_value_full))
+    full_ffn = lax.all_gather(packed_ffn, SHARDS, axis=0, tiled=True)
+    up = full_ffn[:, :hidden_units]
+    down_t = full_ffn[:, hidden_units:]
 
     allowed = []
     probs_all = []
@@ -334,7 +332,7 @@
         attended.append(jnp.concatenate(pieces, axis=1).astype(jnp.bfloat16))
         branch.append(dot("ce,de->cd", attended[b], mix_t))
 
-    branch = tensor_sum(branch, 4, 0)
+    branch = tensor_sum(branch, 8, 0)
     hidden = []
     normals2 = []
     inverses2 = []
@@ -360,7 +358,7 @@
         grad_sum2.append(dot("cf,df->cd", grad_pre[b], up))
     for b in range(micro):
         lifted.append(dot("cf,df->cd", activated[b], down_t))
-    sums = tensor_sum(grad_sum2 + lifted, 4, 1)
+    sums = tensor_sum(grad_sum2 + lifted, 16, 1)
     grad_sum2, lifted = sums[:micro], sums[micro:]
     results = [
         (hidden[b] + lifted[b].astype(jnp.float32) + bias_rows[1]).astype(jnp.bfloat16)
@@ -422,7 +420,7 @@
     for b in range(micro):
         triples.append(jnp.concatenate([query_grads[b], key_value_own[b]], axis=1))
         grad_normed.append(dot("ce,de->cd", triples[b], entry))
-    grad_normed = tensor_sum(grad_normed, 4, 0)
+    grad_normed = tensor_sum(grad_normed, 8, 0)
     triple_all = both(triples)
     grad_hidden_all = both(grad_hidden_b)
     triple_sums = jnp.sum(triple_all.astype(jnp.float32), axis=0)

time: 539 us -> 496 us (0.920)
  Pallas kernels: 259 us -> 200 us
  other arithmetic: 51 us -> 72.6 us
  waiting for transfers between devices: 76.9 us -> 62.6 us
  local copies, waits for them, and re-layouts: 68.7 us -> 80.2 us
    pallas_call x3, Pallas kernels: 259 us -> 200 us  [tensor_sum(): pl.pallas_call(functools.partial(line_sum_kernel, count), out_shape=jax.S...]
    all_gather x1, waiting for transfers between devices: 36.6 us -> 25.3 us  [per_device(): full = lax.all_gather(packed, SHARDS, axis=0, tiled=True)]
    unnamed x283 -> x281, local copies, waits for them, and re-layouts: 29.1 us -> 30.9 us
    unnamed x7 -> x8, waiting for transfers between devices: 22.3 us -> 22.4 us
  transfers between devices with their start and end apart: 5 -> 6, of which waited for: 4 -> 4; matrix products, arithmetic and copies ran while one was open for 16% -> 24% of each run, Pallas kernels for 14% -> 23%
where the time goes in v2:
time: 496 us; the launch traced here: 490 us
  Pallas kernels  200 us (40%)
  local copies, waits for them, and re-layouts  80.2 us (16%)
  other arithmetic  72.6 us (15%)
  waiting for transfers between devices  62.6 us (13%)
  matrix products  57.1 us (12%)
  between operations  16.3 us (3%)
    pallas_call x3, Pallas kernels, tensor_sum(): pl.pallas_call(functools.partial(line_sum_kernel, count), out_shape=jax.S...  200 us
    dot_general x50, matrix products, dot(): return jnp.einsum(equation, left, right, preferred_element_type=jnp.float32)  51.2 us
    unnamed x281, local copies, waits for them, and re-layouts  30.9 us
    all_gather x1, waiting for transfers between devices, per_device(): full = lax.all_gather(packed, SHARDS, axis=0, tiled=True)  25.3 us
    unnamed x8, waiting for transfers between devices  22.4 us
    all_gather x1, waiting for transfers between devices, per_device(): key_value_full = lax.all_gather(key_value, 'seq', axis=1, tiled=True)  14 us
  transfers between devices with their start and end apart: 6, of which 4 were waited for; matrix products, arithmetic and copies ran while one was open for 24% of the time, Pallas kernels for 23%

profile of v2, /device:TPU:0, one launch (start us, length us, event | category | flops | bytes accessed | tf_op | source)
XLA Modules:
  0.0 489.7 jit_solution(15888257254873678858)
XLA Ops:
  14.0 1.6 convert_reduce_fusion.1
  16.4 25.3 %all-gather.4.cloned.1.call-done = bf16[768,896]{1,0:T(8,128)(2,1)} async-done(((bf16[96,896]{1,0:T(8,128)(2,1)}), bf16[768,896]{1,0:T(8,128)(2,1)}) %all-gather.4.cloned.1.call-update) | async-done | bytes 1376272 | tf_op jit(solution)/shard_map/all_gather | solution.py:259
  56.1 1.8 pad_maximum_fusion.10
  57.8 1.9 slice_convert_fusion.8
  62.8 14.0 %all-gather.6.cloned.1.call-done = bf16[2,1024,384]{1,2,0:T(8,128)(2,1)} async-done(((bf16[2,512,384]{1,2,0:T(8,128)(2,1)}), bf16[2,1024,384]{1,2,0:T(8,128)(2,1)}) %all-gather.6.cloned.1.call-update) | async-done | bytes 1572880 | tf_op jit(solution)/shard_map/all_gather | solution.py:304
  82.3 2.1 fusion.294
  91.2 2.2 exponential_reduce_fusion
  100.6 55.0 %line_sum.3 = bf16[8,4,32,768]{3,2,1,0:T(8,128)(2,1)} custom-call(bf16[8,4,32,768]{3,2,1,0:T(8,128)(2,1)} %bitcast.285), custom_call_target="tpu_custom_call" | custom-call | tf_op jit(solution)/shard_map/line_sum/pallas_call | solution.py:185
  160.5 2.8 multiply_reduce_fusion.15
  167.8 3.4 add_convert_fusion.1
  171.2 2.7 multiply_convert_fusion.7
  173.9 2.4 fusion.300
  177.3 2.4 fusion.301
  183.2 2.0 pad_maximum_fusion
  185.2 89.6 %line_sum.4 = bf16[16,4,32,768]{3,2,1,0:T(8,128)(2,1)} custom-call(bf16[16,4,32,768]{3,2,1,0:T(8,128)(2,1)} %bitcast.284), custom_call_target="tpu_custom_call" | custom-call | tf_op jit(solution)/shard_map/line_sum/pallas_call | solution.py:185
  274.7 4.3 convert_reduce_fusion.4
  289.0 4.4 fusion.289
  303.9 2.5 fusion.96
  316.9 3.4 fusion.88
  322.0 4.5 copy.89
  329.3 2.7 fusion.99
  338.6 2.4 slice_convert_fusion.7
  351.9 2.7 convolution_convert_fusion.5
  357.0 55.5 %line_sum.5 = bf16[8,4,32,768]{3,2,1,0:T(8,128)(2,1)} custom-call(bf16[8,4,32,768]{3,2,1,0:T(8,128)(2,1)} %bitcast.286), custom_call_target="tpu_custom_call" | custom-call | tf_op jit(solution)/shard_map/line_sum/pallas_call | solution.py:185
  412.6 3.8 convert_reduce_fusion.2
  431.6 1.7 copy.80
  433.4 2.8 fusion.93
  437.4 2.5 copy.87
  440.4 1.9 slice_convert_fusion.3
  443.3 2.9 fusion.84
  446.2 1.7 fusion.71
  453.6 22.3 %reduce-scatter.10.cloned.1.call-done = bf16[96,896]{1,0:T(8,128)(2,1)} async-done(((bf16[768,896]{1,0:T(8,128)(2,1)}), bf16[96,896]{1,0:T(8,128)(2,1)}) %reduce-scatter.10.cloned.1.call-update) | async-done | bytes 172048
  (497 shorter events, 142.2 us)
Async XLA Ops:
  7.2 8.6 %copy-start = (bf16[2,512,768]{2,1,0:T(8,128)(2,1)S(1)}, bf16[2,512,768]{2,1,0:T(8,128)(2,1)}, u32[]{:S(2)}) copy-start(bf16[2,512,768]{2,1,0:T(8,128)(2,1)} %param.12) | copy-start | bytes 4718596
  7.2 34.5 %all-gather.4.cloned.1.call-start = ((), (), s32[]{:S(2)}) async-start(), calls=%async_computation.3 | async-start | bytes 1548288 | tf_op jit(solution)/shard_map/all_gather | solution.py:259
  14.0 62.8 %all-gather.6.cloned.1.call-start = ((), (), s32[]{:S(2)}) async-start(), calls=%async_computation.4 | async-start | bytes 2359296 | tf_op jit(solution)/shard_map/all_gather | solution.py:304
  15.7 36.0 %copy-start.90 = (f32[512]{0:T(512)}, f32[512]{0:T(512)S(1)}, u32[]{:S(2)}) copy-start(f32[512]{0:T(512)S(1)} %get-tuple-element.188) | copy-start | bytes 6148
  15.7 36.7 %copy-start.88 = (f32[512]{0:T(512)}, f32[512]{0:T(512)S(1)}, u32[]{:S(2)}) copy-start(f32[512]{0:T(512)S(1)} %get-tuple-element.187) | copy-start | bytes 6148
  16.3 34.7 %copy-start.97 = (f32[512]{0:T(512)}, f32[512]{0:T(512)S(1)}, u32[]{:S(2)}) copy-start(f32[512]{0:T(512)S(1)} %add_rsqrt_fusion.2) | copy-start | bytes 6148
  16.4 29.0 %copy-start.99 = (f32[512]{0:T(512)}, f32[512]{0:T(512)S(1)}, u32[]{:S(2)}) copy-start(f32[512]{0:T(512)S(1)} %add_rsqrt_fusion.3) | copy-start | bytes 6148
  49.4 121.7 %all-gather.8.cloned.1.call-start = ((), (), s32[]{:S(2)}) async-start(), calls=%async_computation.5 | async-start | bytes 2654208 | tf_op jit(solution)/shard_map/all_gather | solution.py:307
  78.3 15.2 %copy-start.44 = (bf16[1024,384]{0,1:T(8,128)(2,1)}, bf16[1024,384]{0,1:T(8,128)(2,1)S(1)}, u32[]{:S(2)}) copy-start(bf16[1024,384]{0,1:T(8,128)(2,1)S(1)} %get-tuple-element.132) | copy-start | bytes 2359300
  78.3 18.9 %copy-start.41 = (bf16[1024,384]{0,1:T(8,128)(2,1)}, bf16[1024,384]{0,1:T(8,128)(2,1)S(1)}, u32[]{:S(2)}) copy-start(bf16[1024,384]{0,1:T(8,128)(2,1)S(1)} %get-tuple-element.133) | copy-start | bytes 2359300
  79.1 5.7 %copy-start.16 = (f32[512,1024]{1,0:T(8,128)}, f32[512,1024]{1,0:T(8,128)S(1)}, u32[]{:S(2)}) copy-start(f32[512,1024]{1,0:T(8,128)S(1)} %get-tuple-element.166) | copy-start | bytes 6291460
  79.9 6.7 %copy-start.14 = (f32[512,1024]{1,0:T(8,128)}, f32[512,1024]{1,0:T(8,128)S(1)}, u32[]{:S(2)}) copy-start(f32[512,1024]{1,0:T(8,128)S(1)} %get-tuple-element.164) | copy-start | bytes 6291460
  80.7 7.1 %copy-start.11 = (f32[512,1024]{1,0:T(8,128)}, f32[512,1024]{1,0:T(8,128)S(1)}, u32[]{:S(2)}) copy-start(f32[512,1024]{1,0:T(8,128)S(1)} %get-tuple-element.162) | copy-start | bytes 6291460
  81.5 7.4 %copy-start.8 = (f32[512,1024]{1,0:T(8,128)}, f32[512,1024]{1,0:T(8,128)S(1)}, u32[]{:S(2)}) copy-start(f32[512,1024]{1,0:T(8,128)S(1)} %get-tuple-element.160) | copy-start | bytes 6291460
  82.3 7.2 %copy-start.5 = (f32[512,1024]{1,0:T(8,128)}, f32[512,1024]{1,0:T(8,128)S(1)}, u32[]{:S(2)}) copy-start(f32[512,1024]{1,0:T(8,128)S(1)} %get-tuple-element.158) | copy-start | bytes 6291460
  84.4 6.2 %copy-start.117 = (f32[512]{0:T(512)}, f32[512]{0:T(512)S(1)}, u32[]{:S(2)}) copy-start(f32[512]{0:T(512)S(1)} %get-tuple-element.155) | copy-start | bytes 6148
  89.4 6.0 %copy-start.75 = (f32[512]{0:T(512)}, f32[512]{0:T(512)S(1)}, u32[]{:S(2)}) copy-start(f32[512]{0:T(512)S(1)} %log_add_fusion.2) | copy-start | bytes 6148
  91.2 250.7 %reduce-scatter.8.cloned.1.call-start = ((), (), s32[]{:S(2)}) async-start(), calls=%async_computation.6 | async-start | bytes 2359296 | tf_op jit(solution)/shard_map/reduce_scatter | solution.py:414
  173.8 7.7 %copy-start.128 = (bf16[512,768]{1,0:T(8,128)(2,1)}, bf16[512,768]{1,0:T(8,128)(2,1)S(1)}, u32[]{:S(2)}) copy-start(bf16[512,768]{1,0:T(8,128)(2,1)S(1)} %get-tuple-element.169) | copy-start | bytes 2359300
  316.6 133.9 %reduce-scatter.12.cloned.1.call-start = ((), (), s32[]{:S(2)}) async-start(), calls=%async_computation.8 | async-start | bytes 2654208
  321.9 5.3 %copy-start.108 = (f32[768]{0:T(1024)S(1)}, f32[768]{0:T(1024)}, u32[]{:S(2)}) copy-start(f32[768]{0:T(1024)} %get-tuple-element.117) | copy-start | bytes 9220
  321.9 5.9 %copy-start.105 = (f32[768]{0:T(1024)S(1)}, f32[768]{0:T(1024)}, u32[]{:S(2)}) copy-start(f32[768]{0:T(1024)} %get-tuple-element.71) | copy-start | bytes 9220
  321.9 5.9 %copy-start.106 = (f32[768]{0:T(1024)S(1)}, f32[768]{0:T(1024)}, u32[]{:S(2)}) copy-start(f32[768]{0:T(1024)} %get-tuple-element.72) | copy-start | bytes 9220
  321.9 6.6 %copy-start.120 = (bf16[768]{0:T(1024)(128)(2,1)S(1)}, bf16[768]{0:T(1024)(128)(2,1)}, u32[]{:S(2)}) copy-start(bf16[768]{0:T(1024)(128)(2,1)} %get-tuple-element.183) | copy-start | bytes 4612
  321.9 6.6 %copy-start.121 = (bf16[768]{0:T(1024)(128)(2,1)S(1)}, bf16[768]{0:T(1024)(128)(2,1)}, u32[]{:S(2)}) copy-start(bf16[768]{0:T(1024)(128)(2,1)} %get-tuple-element.185) | copy-start | bytes 4612
  321.9 7.4 %copy-start.65 = (bf16[512,64]{0,1:T(8,128)(2,1)S(1)}, bf16[512,64]{0,1:T(8,128)(2,1)}, u32[]{:S(2)}) copy-start(bf16[512,64]{0,1:T(8,128)(2,1)} %convolution_convert_fusion.21) | copy-start | bytes 196612
  321.9 7.4 %copy-start.67 = (bf16[512,64]{0,1:T(8,128)(2,1)S(1)}, bf16[512,64]{0,1:T(8,128)(2,1)}, u32[]{:S(2)}) copy-start(bf16[512,64]{0,1:T(8,128)(2,1)} %convolution_convert_fusion.20) | copy-start | bytes 196612
  321.9 7.4 %copy-start.69 = (bf16[512,64]{0,1:T(8,128)(2,1)S(1)}, bf16[512,64]{0,1:T(8,128)(2,1)}, u32[]{:S(2)}) copy-start(bf16[512,64]{0,1:T(8,128)(2,1)} %copy-done.68) | copy-start | bytes 196612
  321.9 7.4 %copy-start.71 = (bf16[512,64]{0,1:T(8,128)(2,1)S(1)}, bf16[512,64]{0,1:T(8,128)(2,1)}, u32[]{:S(2)}) copy-start(bf16[512,64]{0,1:T(8,128)(2,1)} %copy-done.70) | copy-start | bytes 196612
  321.9 7.3 %copy-start.73 = (bf16[512,64]{0,1:T(8,128)(2,1)S(1)}, bf16[512,64]{0,1:T(8,128)(2,1)}, u32[]{:S(2)}) copy-start(bf16[512,64]{0,1:T(8,128)(2,1)} %copy-done.72) | copy-start | bytes 196612
  329.3 6.0 %copy-start.43 = (bf16[1024,384]{0,1:T(8,128)(2,1)S(1)}, bf16[1024,384]{0,1:T(8,128)(2,1)}, u32[]{:S(2)}) copy-start(bf16[1024,384]{0,1:T(8,128)(2,1)} %copy-done.41) | copy-start | bytes 2359300
  341.0 134.8 %reduce-scatter.10.cloned.1.call-start = ((), (), s32[]{:S(2)}) async-start(), calls=%async_computation.7 | async-start | bytes 1548288
  (106 other events, 260.2 us)
Sparse Core Ops, SparseCore 0:
  14.1 27.5 all-gather.3
  49.6 27.2 all-gather.5
  91.3 29.0 all-gather.7
  316.7 25.1 reduce-scatter.7
  345.4 42.5 reduce-scatter.11
  440.1 35.6 reduce-scatter.9
